TPU v7x, 128 devices: a whole 4x4x4 slice. The times are simulated.
128 devices in a mesh: seq: 32 (over y, x, core), hid: 4 (over z).
Axes of the slice: x: 4, y: 4, z: 4, core: 2. Of those that a mesh axis runs over, the one named last changes fastest.
Arguments:
- patches: bfloat16 [12288, 3200], P('seq'), may hold values from -6 to 6
- norm_gain: float32 [3200], replicated, may hold values from 0.5 to 8
- query_weight: bfloat16 [3200, 2048], P(None, 'hid'), may hold values from -0.109375 to 0.109375
- key_weight: bfloat16 [3200, 2048], P(None, 'hid'), may hold values from -0.7424621 to 0.7424621
- value_weight: bfloat16 [3200, 2048], P(None, 'hid'), may hold values from -0.109375 to 0.109375
- out_weight: bfloat16 [2048, 3200], P('hid'), may hold values from -0.125 to 0.125
- layer_scale: float32 [3200], replicated, may hold values from 0.3 to 1.5
- merge_gain: float32 [12800], P('hid'), may hold values from 0.5 to 1.5
- merge_bias: float32 [12800], P('hid'), may hold values from -3 to 3
- proj_weight: bfloat16 [12800, 6144], P('hid', 'seq'), may hold values from -0.0546875 to 0.0546875
- proj_bias: float32 [6144], P('seq'), may hold values from -3 to 3
- text_rows: bfloat16 [512, 6144], P(None, 'seq'), may hold values from -6 to 6
- stream_gain: float32 [6144], P('hid'), may hold values from 0.5 to 1.5
- tile_counts: int32 [3], replicated, may hold values from 1 to 7, as said below
- image_slots: int32 [3072], replicated, may hold values from 0 to 3583, as said below
- text_slots: int32 [512], replicated, may hold values from 0 to 3583, as said below
Outputs:
- stream: bfloat16 [3584, 6144], P('seq', 'hid')
- normed: bfloat16 [3584, 6144], P('seq', 'hid')
Inputs may be any that keep to these rules, and one draw needn't show every extreme that they name: `tile_counts`: the tile counts sum to 12; the largest is exactly 7. `image_slots`: image slots and text slots together name every stream position once; each image's rows lie in order at consecutive positions. `text_slots`: see image_slots; text slots increase.
All inputs are finite; a program needn't handle non-finite values.
Results may differ from a plain program's by a relative error of at most 0.022.
The roundings to bfloat16 on the way count: a program that leaves them out, or rounds other values in their place, can miss the bound.
Values may be sent and summed in bfloat16 or wider, within the bound.
No kernel may reach another device: no remote copies, remote signals or barrier semaphores. Data moves between devices by JAX's collectives and lax.ppermute only.
A program may use at most 192 MiB of HBM per device.

v0:
```python
import jax
import jax.numpy as jnp
from jax import lax
from jax.sharding import PartitionSpec as P

HD = 128
SIDE = 32


def image_of(index_rows, tile_counts):
    bounds = jnp.cumsum(tile_counts) * (SIDE * SIDE)
    return jnp.sum((index_rows[:, None] >= bounds[None, :]).astype(jnp.int32), axis=1)


def shuffle_rows(values):
    row_count, width = values.shape
    grouped = values.reshape(row_count // (2 * SIDE), 2, SIDE // 2, 2, width)
    return grouped.transpose(0, 2, 4, 1, 3).reshape(row_count // 4, 4 * width)


def per_device(
    patches,
    norm_gain,
    query_weight,
    key_weight,
    value_weight,
    out_weight,
    layer_scale,
    merge_gain,
    merge_bias,
    proj_weight,
    proj_bias,
    text_rows,
    stream_gain,
    tile_counts,
    image_slots,
    text_slots,
):
    seq_index = lax.axis_index("seq")
    hid_index = lax.axis_index("hid")
    local_rows = patches.shape[0]
    local_heads = query_weight.shape[1] // HD
    tokens_f = patches.astype(jnp.float32)
    normed_in = (
        tokens_f * lax.rsqrt(jnp.mean(tokens_f * tokens_f, -1, keepdims=True) + 1e-06) * norm_gain
    ).astype(jnp.bfloat16)
    queries = (
        jnp.dot(normed_in, query_weight, preferred_element_type=jnp.float32) * HD ** (-0.5)
    ).astype(jnp.bfloat16)
    key_rows = jnp.dot(normed_in, key_weight, preferred_element_type=jnp.float32).astype(
        jnp.bfloat16
    )
    value_rows = jnp.dot(normed_in, value_weight, preferred_element_type=jnp.float32).astype(
        jnp.bfloat16
    )
    query_heads = queries.reshape(local_rows, local_heads, HD)
    query_ids = image_of(
        seq_index * local_rows + jnp.arange(local_rows, dtype=jnp.int32), tile_counts
    )

    def fold_block(state_now, key_block, value_block, block_start):
        maxima, totals, accumulated = state_now
        row_count = key_block.shape[0]
        key_heads = key_block.reshape(row_count, local_heads, HD)
        value_heads = value_block.reshape(row_count, local_heads, HD)
        scores = jnp.einsum(
            "qhd,khd->hqk", query_heads, key_heads, preferred_element_type=jnp.float32
        )
        key_ids = image_of(block_start + jnp.arange(row_count, dtype=jnp.int32), tile_counts)
        same_image = (query_ids[:, None] == key_ids[None, :])[None]
        scores = jnp.where(same_image, scores, jnp.float32(-1e30))
        new_max = jnp.maximum(maxima, jnp.max(scores, axis=-1))
        factor = jnp.exp(maxima - new_max)
        weights = jnp.where(same_image, jnp.exp(scores - new_max[..., None]), jnp.float32(0.0))
        totals = totals * factor + jnp.sum(weights, axis=-1)
        update = jnp.einsum(
            "hqk,khd->hqd",
            weights.astype(jnp.bfloat16),
            value_heads,
            preferred_element_type=jnp.float32,
        )
        accumulated = accumulated * factor[..., None] + update
        return (new_max, totals, accumulated)

    start_state = (
        jnp.full((local_heads, local_rows), -1e30, jnp.float32),
        jnp.zeros((local_heads, local_rows), jnp.float32),
        jnp.zeros((local_heads, local_rows, HD), jnp.float32),
    )
    key_piece = lax.all_gather(key_rows, "seq", axis=0, tiled=True)
    value_piece = lax.all_gather(value_rows, "seq", axis=0, tiled=True)
    row_count = key_piece.shape[0]
    block_rows = 512
    steps_count = row_count // block_rows
    key_blocks = key_piece.reshape(steps_count, block_rows, key_piece.shape[1])
    value_blocks = value_piece.reshape(steps_count, block_rows, value_piece.shape[1])

    def step_fn(state_in, inputs):
        key_block, value_block, index_now = inputs
        return (fold_block(state_in, key_block, value_block, index_now * block_rows), None)

    result, unused = lax.scan(
        step_fn, start_state, (key_blocks, value_blocks, jnp.arange(steps_count, dtype=jnp.int32))
    )
    maxima, totals, accumulated = result
    attended = (accumulated / totals[..., None]).astype(jnp.bfloat16)
    attended = attended.transpose(1, 0, 2).reshape(local_rows, local_heads * HD)
    branch_part = jnp.dot(attended, out_weight, preferred_element_type=jnp.float32)
    branch = lax.psum(branch_part.astype(jnp.bfloat16), "hid").astype(jnp.float32)
    merged = shuffle_rows(tokens_f + layer_scale * branch)
    mean_row = jnp.mean(merged, -1, keepdims=True)
    var_row = jnp.mean(merged * merged, -1, keepdims=True) - mean_row * mean_row
    block_width = merged.shape[1] // lax.axis_size("hid")
    merged_block = lax.dynamic_slice_in_dim(merged, hid_index * block_width, block_width, 1)
    merged_normed = (
        (merged_block - mean_row) * lax.rsqrt(var_row + 1e-05) * merge_gain + merge_bias
    ).astype(jnp.bfloat16)
    partial_proj = jnp.dot(
        lax.all_gather(merged_normed, "seq", axis=0, tiled=True),
        proj_weight,
        preferred_element_type=jnp.float32,
    )
    stream_size = image_slots.shape[0] + text_slots.shape[0]
    summed = lax.psum(partial_proj.astype(jnp.bfloat16), "hid").astype(jnp.float32)
    image_rows = jax.nn.gelu(summed + proj_bias, approximate=False).astype(jnp.bfloat16)
    stream_cols = (
        jnp.zeros((stream_size, image_rows.shape[1]), jnp.bfloat16)
        .at[image_slots]
        .set(image_rows)
        .at[text_slots]
        .set(text_rows)
    )
    stream_full = lax.all_to_all(stream_cols, "seq", split_axis=0, concat_axis=1, tiled=True)
    stream_f = stream_full.astype(jnp.float32)
    inverse_rms = lax.rsqrt(jnp.mean(stream_f * stream_f, -1, keepdims=True) + 1e-05)
    out_width = stream_full.shape[1] // lax.axis_size("hid")
    stream_share = lax.dynamic_slice_in_dim(stream_full, hid_index * out_width, out_width, 1)
    normed_share = (stream_share.astype(jnp.float32) * inverse_rms * stream_gain).astype(
        jnp.bfloat16
    )
    return (stream_share, normed_share)


def solution(mesh):
    return jax.shard_map(
        per_device,
        mesh=mesh,
        in_specs=(
            P("seq", None),
            P(),
            P(None, "hid"),
            P(None, "hid"),
            P(None, "hid"),
            P("hid", None),
            P(),
            P("hid"),
            P("hid"),
            P("hid", "seq"),
            P("seq"),
            P(None, "seq"),
            P("hid"),
            P(),
            P(),
            P(),
        ),
        out_specs=(P("seq", "hid"), P("seq", "hid")),
        check_vma=False,
    )
```

profile of v0, /device:TPU:0, one launch (start us, length us, event | category | flops | bytes accessed | tf_op | source)
XLA Modules:
  0.0 976.0 jit_solution(10442808038477700343)
XLA Ops:
  14.1 5.0 convolution_convert_fusion.2
  24.6 54.9 %all-gather.4.cloned.1.call-done = bf16[12288,512]{1,0:T(8,128)(2,1)} async-done(((bf16[384,512]{1,0:T(8,128)(2,1)}), bf16[12288,512]{1,0:T(8,128)(2,1)}) %all-gather.4.cloned.1.call-update) | async-done | bytes 12582928 | tf_op jit(solution)/shard_map/all_gather | solution.py:90
  79.5 64.6 %all-gather.6.cloned.1.call-done = bf16[12288,512]{1,0:T(8,128)(2,1)} async-done(((bf16[384,512]{1,0:T(8,128)(2,1)}), bf16[12288,512]{1,0:T(8,128)(2,1)}) %all-gather.6.cloned.1.call-update) | async-done | bytes 12582928 | tf_op jit(solution)/shard_map/all_gather | solution.py:91
  144.1 443.7 %while.17 = (s32[]{:T(128)}, f32[4,384]{1,0:T(4,128)S(1)}, f32[4,384]{1,0:T(4,128)S(1)}, f32[4,384,128]{2,1,0:T(8,128)}, s32[384]{0:T(512)S(1)}, /*index=5*/s32[...) while((s32[]{:T(128)}, f32[4,384]{1,0:T(4,128)S(1)}, ...), condition=%wide.region_7.8_spmd.clone, body=%wide.region_3.7_spmd.clone.sunk | while | flops 411316224 | bytes 17540812 | solution.py:102
  176.6 4.3 fusion.63
  213.6 4.3 fusion.63
  232.1 4.3 fusion.63
  269.1 4.3 fusion.63
  306.1 4.3 fusion.63
  324.6 4.3 fusion.63
  361.6 4.3 fusion.63
  380.1 4.3 fusion.63
  417.1 4.3 fusion.63
  454.1 4.3 fusion.63
  472.6 4.3 fusion.63
  491.1 4.3 fusion.63
  509.6 4.3 fusion.63
  528.1 4.3 fusion.63
  565.1 4.3 fusion.63
  594.5 64.3 %all-reduce.3.cloned.1.call-done = bf16[384,3200]{1,0:T(8,128)(2,1)} async-done(((bf16[384,3200]{1,0:T(8,128)(2,1)}), bf16[384,3200]{1,0:T(8,128)(2,1)}) %all-reduce.3.cloned.1.call-update) | async-done | bytes 2457616 | tf_op jit(solution)/shard_map/psum | solution.py:109
  658.9 4.5 convert_add_fusion
  663.4 6.8 reshape.161
  670.2 39.8 %copy.71 = f32[6,2,16,2,3200]{2,0,3,1,4:T(8,128)} copy(f32[6,2,16,2,3200]{4,3,2,1,0:T(2,128)} %reshape.161) | data formatting | bytes 9830400 | tf_op jit(solution)/shard_map/reshape | solution.py:17
  709.9 17.3 %bitcast_reduce_fusion = (f32[6,16]{1,0:T(8,128)S(1)}, f32[6,16]{1,0:T(8,128)S(1)}) fusion(f32[6,2,16,2,3200]{2,0,3,1,4:T(8,128)} %copy.71), kind=kLoop, calls=%fused_computation.81 | loop fusion | flops 3686208 | bytes 4915968 | tf_op jit(solution)/shard_map/reduce_sum | solution.py:111
  727.4 31.2 %reshape.162 = f32[96,12800]{0,1:T(8,128)} reshape(f32[6,16,3200,2,2]{1,0,4,3,2:T(8,128)} %bitcast.71) | data formatting | bytes 9830400 | tf_op jit(solution)/shard_map/reshape | solution.py:18
  761.8 78.9 %all-gather.8.cloned.1.call-done = bf16[3072,3200]{1,0:T(8,128)(2,1)} async-done(((bf16[96,3200]{1,0:T(8,128)(2,1)}), bf16[3072,3200]{1,0:T(8,128)(2,1)}) %all-gather.8.cloned.1.call-update) | async-done | bytes 19660816 | tf_op jit(solution)/shard_map/all_gather | solution.py:119
  840.7 14.4 %convolution_convert_fusion.1 = bf16[3072,192]{0,1:T(8,128)(2,1)} fusion(bf16[3072,3200]{1,0:T(8,128)(2,1)} %all-gather.8.cloned.1.call-done, bf16[3200,192]{0,1:T(8,128)(2,1)} %param.27), kind=kOutput, calls=%fused_computation.34 | convolution fusion | flops 3775463424 | bytes 22069248 | tf_op jit(solution)/shard_map/dot_general | solution.py:118
  855.3 46.3 %all-reduce.5.cloned.1.call-done = bf16[3072,192]{0,1:T(8,128)(2,1)} async-done(((bf16[3072,192]{0,1:T(8,128)(2,1)}), bf16[3072,192]{0,1:T(8,128)(2,1)}) %all-reduce.5.cloned.1.call-update) | async-done | bytes 1179664 | tf_op jit(solution)/shard_map/psum | solution.py:124
  901.6 6.4 fusion.20
  909.6 14.5 %scatter_custom_fusion = bf16[3584,192]{1,0:T(8,128)(2,1)S(1)} fusion(s32[3072]{0:T(1024)S(1)} %compare_select_fusion, bf16[3072,192]{1,0:T(8,128)(2,1)} %copy.73, bf16[]{:T(256)} %constant.65.clone.1), kind=kCustom, calls=%fused_computation.64 | custom fusion | bytes 1376768 | tf_op jit(solution)/shard_map/scatter | solution.py:129
  930.0 7.3 all-to-all-start
  937.4 23.9 %all-to-all-done = bf16[32,112,192]{1,2,0:T(8,128)(2,1)} async-done(((bf16[32,112,192]{1,2,0:T(8,128)(2,1)}), bf16[32,112,192]{1,2,0:T(8,128)(2,1)}, u32[]{:S(2)}, u32[]{:S(2)}) %all-to-all-start) | async-done | bytes 1376288 | tf_op jit(solution)/shard_map/all_to_all | solution.py:133
  (393 shorter events, 401.5 us)
Async XLA Ops:
  7.2 584.1 %copy-start = (bf16[512,3200]{1,0:T(8,128)(2,1)S(1)}, bf16[512,3200]{1,0:T(8,128)(2,1)}, u32[]{:S(2)}) copy-start(bf16[512,3200]{1,0:T(8,128)(2,1)} %param.23) | copy-start | bytes 9830404
  7.2 72.3 %all-gather.4.cloned.1.call-start = ((), (), s32[]{:S(2)}) async-start(), calls=%async_computation.1 | async-start | bytes 12976128 | tf_op jit(solution)/shard_map/all_gather | solution.py:90
  7.2 2.6 copy-start.2
  9.8 4.3 copy-start.12
  14.1 130.0 %all-gather.6.cloned.1.call-start = ((), (), s32[]{:S(2)}) async-start(), calls=%async_computation.2 | async-start | bytes 12976128 | tf_op jit(solution)/shard_map/all_gather | solution.py:91
  19.2 639.7 %all-reduce.3.cloned.1.call-start = ((), (), s32[]{:S(2)}) async-start(), calls=%async_computation.3 | async-start | bytes 4915200 | tf_op jit(solution)/shard_map/psum | solution.py:109
  19.2 5.1 copy-start.13
  591.3 67.6 %copy-start.5 = (f32[3200]{0:T(1024)S(1)}, f32[3200]{0:T(1024)}, u32[]{:S(2)}) copy-start(f32[3200]{0:T(1024)} %param.24) | copy-start | bytes 38404
  594.3 64.6 %copy-start.3 = (bf16[384,3200]{1,0:T(8,128)(2,1)S(1)}, bf16[384,3200]{1,0:T(8,128)(2,1)}, u32[]{:S(2)}) copy-start(bf16[384,3200]{1,0:T(8,128)(2,1)} %param.18) | copy-start | bytes 7372804
  594.3 246.4 %all-gather.8.cloned.1.call-start = ((), (), s32[]{:S(2)}) async-start(), calls=%async_computation.4 | async-start | bytes 20275200 | tf_op jit(solution)/shard_map/all_gather | solution.py:119
  758.5 2.1 copy-start.6
  758.5 2.1 copy-start.7
  761.7 93.4 %copy-start.4 = (bf16[512,192]{0,1:T(8,128)(2,1)S(1)}, bf16[512,192]{0,1:T(8,128)(2,1)}, u32[]{:S(2)}) copy-start(bf16[512,192]{0,1:T(8,128)(2,1)} %param.29) | copy-start | bytes 589828
  761.8 93.6 %copy-start.10 = (s32[512]{0:T(512)S(1)}, s32[512]{0:T(512)}, u32[]{:S(2)}) copy-start(s32[512]{0:T(512)} %param.33) | copy-start | bytes 6148
  761.8 93.6 %copy-start.8 = (s32[3072]{0:T(1024)S(1)}, s32[3072]{0:T(1024)}, u32[]{:S(2)}) copy-start(s32[3072]{0:T(1024)} %param.32) | copy-start | bytes 36868
  761.8 139.8 %copy-start.11 = (f32[192]{0:T(256)S(1)}, f32[192]{0:T(256)}, u32[]{:S(2)}) copy-start(f32[192]{0:T(256)} %param.28) | copy-start | bytes 2308
  761.8 139.8 %all-reduce.5.cloned.1.call-start = ((), (), s32[]{:S(2)}) async-start(), calls=%async_computation.5 | async-start | bytes 2359296 | tf_op jit(solution)/shard_map/psum | solution.py:124
  930.0 33.5 %copy-start.9 = (f32[1536]{0:T(1024)S(1)}, f32[1536]{0:T(1024)}, u32[]{:S(2)}) copy-start(f32[1536]{0:T(1024)} %param.30) | copy-start | bytes 18436
  930.0 31.3 %all-to-all-start = ((bf16[32,112,192]{1,2,0:T(8,128)(2,1)}), bf16[32,112,192]{1,2,0:T(8,128)(2,1)}, u32[]{:S(2)}, u32[]{:S(2)}) async-start(bf16[32,112,192]{1,2,0:T(8,128)(2,1)} %copy.76), calls=%async_computation | async-start | bytes 3145728 | tf_op jit(solution)/shard_map/all_to_all | solution.py:133
  937.4 32.1 %copy-start.1 = (bf16[512,3200]{1,0:T(8,128)(2,1)S(1)}, bf16[512,3200]{1,0:T(8,128)(2,1)}, u32[]{:S(2)}) copy-start(bf16[512,3200]{1,0:T(8,128)(2,1)} %param.23) | copy-start | bytes 9830404
Sparse Core Ops, SparseCore 0:
  14.2 65.2 all-gather.3
  81.7 62.3 all-gather.5
  594.4 64.4 all-reduce.2
  761.9 78.7 all-gather.7
  855.3 46.2 all-reduce.4
where the time goes:
time: 982 us; the launch traced here: 976 us
  waiting for transfers between devices  333 us (34%)
  local copies, waits for them, and re-layouts  279 us (28%)
  matrix products  220 us (22%)
  other arithmetic  106 us (11%)
  loops' own time  16.4 us (2%)
  between operations  14 us (1%)
    dynamic_slice x96, local copies, waits for them, and re-layouts, per_device(): lax.scan(step_fn, start_state, (key_blocks, value_blocks, jnp.arange(step...  169 us
    dot_general x24, matrix products, fold_block(): jnp.einsum('hqk,khd->hqd', weights.astype(jnp.bfloat16), value_heads, pre...  102 us
    dot_general x24, matrix products, fold_block(): jnp.einsum('qhd,khd->hqk', query_heads, key_heads, preferred_element_type...  87.1 us
    all_gather x1, waiting for transfers between devices, per_device(): lax.all_gather(merged_normed, 'seq', axis=0, tiled=True)  78.9 us
    all_gather x1, waiting for transfers between devices, per_device(): value_piece = lax.all_gather(value_rows, 'seq', axis=0, tiled=True)  64.6 us
    psum x1, waiting for transfers between devices, per_device(): lax.psum(branch_part.astype(jnp.bfloat16), 'hid').astype(jnp.float32)  64.3 us
    reduce_sum x24, other arithmetic, fold_block(): totals = totals * factor + jnp.sum(weights, axis=-1)  61.6 us
    all_gather x1, waiting for transfers between devices, per_device(): key_piece = lax.all_gather(key_rows, 'seq', axis=0, tiled=True)  54.9 us
  transfers between devices with their start and end apart: 6, of which 6 were waited for; matrix products, arithmetic and copies ran while one was open for 1% of the time, Pallas kernels for 0%

commit v1 on v0

--- a/solution.py
+++ b/solution.py
@@ -88,7 +88,11 @@
         jnp.zeros((local_heads, local_rows, HD), jnp.float32),
     )
     key_piece = lax.all_gather(key_rows, "seq", axis=0, tiled=True)
-    value_piece = lax.all_gather(value_rows, "seq", axis=0, tiled=True)
+    peers = lax.axis_size("seq")
+    repeats = [peers if d == 0 else 1 for d in range(value_rows.ndim)]
+    value_piece = lax.all_to_all(
+        jnp.tile(value_rows, repeats), "seq", split_axis=0, concat_axis=0, tiled=True
+    )
     row_count = key_piece.shape[0]
     block_rows = 512
     steps_count = row_count // block_rows

time: 982 us -> 1050 us (1.069)
  waiting for transfers between devices: 333 us -> 386 us
    all_to_all x0 -> x1, waiting for transfers between devices: none -> 171 us  [per_device(): lax.all_to_all(jnp.tile(value_rows, repeats), 'seq', split_axis=0, concat...]
    all_gather x1 -> x0, waiting for transfers between devices: 64.6 us -> none  [per_device(): value_piece = lax.all_gather(value_rows, 'seq', axis=0, tiled=True)]
    all_gather x1, waiting for transfers between devices: 54.9 us -> 0.01 us  [per_device(): key_piece = lax.all_gather(key_rows, 'seq', axis=0, tiled=True)]
  transfers between devices with their start and end apart: 6 -> 6, of which waited for: 6 -> 5; matrix products, arithmetic and copies ran while one was open for 1% -> 2% of each run, Pallas kernels for 0% -> 0%
where the time goes in v1:
time: 1050 us; the launch traced here: 1040 us
  waiting for transfers between devices  386 us (37%)
  local copies, waits for them, and re-layouts  283 us (27%)
  matrix products  220 us (21%)
  other arithmetic  106 us (10%)
  loops' own time  16.4 us (2%)
  starting transfers between devices  15.2 us (1%)
  between operations  14 us (1%)
    all_to_all x1, waiting for transfers between devices, per_device(): lax.all_to_all(jnp.tile(value_rows, repeats), 'seq', split_axis=0, concat...  171 us
    dynamic_slice x96, local copies, waits for them, and re-layouts, per_device(): lax.scan(step_fn, start_state, (key_blocks, value_blocks, jnp.arange(step...  168 us
    dot_general x24, matrix products, fold_block(): jnp.einsum('hqk,khd->hqd', weights.astype(jnp.bfloat16), value_heads, pre...  102 us
    dot_general x24, matrix products, fold_block(): jnp.einsum('qhd,khd->hqk', query_heads, key_heads, preferred_element_type...  87.5 us
    all_gather x1, waiting for transfers between devices, per_device(): lax.all_gather(merged_normed, 'seq', axis=0, tiled=True)  78.9 us
    psum x1, waiting for transfers between devices, per_device(): lax.psum(branch_part.astype(jnp.bfloat16), 'hid').astype(jnp.float32)  65.7 us
    reduce_sum x24, other arithmetic, fold_block(): totals = totals * factor + jnp.sum(weights, axis=-1)  61.6 us
    reshape x2, local copies, waits for them, and re-layouts, shuffle_rows(): grouped = values.reshape(row_count // (2 * SIDE), 2, SIDE // 2, 2, width)  46.5 us
  transfers between devices with their start and end apart: 6, of which 5 were waited for; matrix products, arithmetic and copies ran while one was open for 2% of the time, Pallas kernels for 0%

profile of v1, /device:TPU:0, one launch (start us, length us, event | category | flops | bytes accessed | tf_op | source)
XLA Modules:
  0.0 1040.6 jit_solution(4683728854000141110)
XLA Ops:
  18.3 6.0 tile.2
  24.3 7.5 all-to-all-start
  31.9 4.3 fusion.32
  37.4 171.3 %all-to-all-done = bf16[32,384,512]{2,1,0:T(8,128)(2,1)} async-done(((bf16[32,384,512]{2,1,0:T(8,128)(2,1)}), bf16[32,384,512]{2,1,0:T(8,128)(2,1)}, u32[]{:S(2)}, u32[]{:S(2)}) %all-to-all-start) | async-done | bytes 12582944 | tf_op jit(solution)/shard_map/all_to_all | solution.py:93
  208.7 442.4 %while.17 = (s32[]{:T(128)}, f32[4,384]{1,0:T(4,128)S(1)}, f32[4,384]{1,0:T(4,128)S(1)}, f32[4,384,128]{2,1,0:T(8,128)}, s32[384]{0:T(512)S(1)}, /*index=5*/s32[...) while((s32[]{:T(128)}, f32[4,384]{1,0:T(4,128)S(1)}, ...), condition=%wide.region_7.8_spmd.clone, body=%wide.region_3.7_spmd.clone.sunk | while | flops 411316224 | bytes 17540812 | solution.py:106
  241.1 4.3 fusion.63
  259.5 4.3 fusion.63
  278.0 4.3 fusion.63
  296.4 4.3 fusion.63
  370.2 4.3 fusion.63
  388.6 4.3 fusion.63
  407.1 4.3 fusion.63
  425.5 4.3 fusion.63
  443.9 4.3 fusion.63
  536.2 4.3 fusion.63
  554.6 4.3 fusion.63
  573.0 4.3 fusion.63
  591.5 4.3 fusion.63
  609.9 4.3 fusion.63
  657.8 65.7 %all-reduce.3.cloned.1.call-done = bf16[384,3200]{1,0:T(8,128)(2,1)} async-done(((bf16[384,3200]{1,0:T(8,128)(2,1)}), bf16[384,3200]{1,0:T(8,128)(2,1)}) %all-reduce.3.cloned.1.call-update) | async-done | bytes 2457616 | tf_op jit(solution)/shard_map/psum | solution.py:113
  723.6 4.5 convert_add_fusion
  728.1 6.7 reshape.169
  734.8 39.8 %copy.84 = f32[6,2,16,2,3200]{2,0,3,1,4:T(8,128)} copy(f32[6,2,16,2,3200]{4,3,2,1,0:T(2,128)} %reshape.169) | data formatting | bytes 9830400 | tf_op jit(solution)/shard_map/reshape | solution.py:17
  774.6 17.3 %bitcast_reduce_fusion = (f32[6,16]{1,0:T(8,128)S(1)}, f32[6,16]{1,0:T(8,128)S(1)}) fusion(f32[6,2,16,2,3200]{2,0,3,1,4:T(8,128)} %copy.84), kind=kLoop, calls=%fused_computation.81 | loop fusion | flops 3686208 | bytes 4915968 | tf_op jit(solution)/shard_map/reduce_sum | solution.py:115
  792.0 31.2 %reshape.170 = f32[96,12800]{0,1:T(8,128)} reshape(f32[6,16,3200,2,2]{1,0,4,3,2:T(8,128)} %bitcast.71) | data formatting | bytes 9830400 | tf_op jit(solution)/shard_map/reshape | solution.py:18
  826.5 78.9 %all-gather.5.cloned.1.call-done = bf16[3072,3200]{1,0:T(8,128)(2,1)} async-done(((bf16[96,3200]{1,0:T(8,128)(2,1)}), bf16[3072,3200]{1,0:T(8,128)(2,1)}) %all-gather.5.cloned.1.call-update) | async-done | bytes 19660816 | tf_op jit(solution)/shard_map/all_gather | solution.py:123
  905.4 14.4 %convolution_convert_fusion.1 = bf16[3072,192]{0,1:T(8,128)(2,1)} fusion(bf16[3072,3200]{1,0:T(8,128)(2,1)} %all-gather.5.cloned.1.call-done, bf16[3200,192]{0,1:T(8,128)(2,1)} %param.27), kind=kOutput, calls=%fused_computation.34 | convolution fusion | flops 3775463424 | bytes 22069248 | tf_op jit(solution)/shard_map/dot_general | solution.py:122
  920.0 46.2 %all-reduce.5.cloned.1.call-done = bf16[3072,192]{0,1:T(8,128)(2,1)} async-done(((bf16[3072,192]{0,1:T(8,128)(2,1)}), bf16[3072,192]{0,1:T(8,128)(2,1)}) %all-reduce.5.cloned.1.call-update) | async-done | bytes 1179664 | tf_op jit(solution)/shard_map/psum | solution.py:128
  966.3 6.4 fusion.20
  974.3 14.5 %scatter_custom_fusion = bf16[3584,192]{1,0:T(8,128)(2,1)S(1)} fusion(s32[3072]{0:T(1024)S(1)} %compare_select_fusion, bf16[3072,192]{1,0:T(8,128)(2,1)} %copy.86, bf16[]{:T(256)} %constant.65.clone.1), kind=kCustom, calls=%fused_computation.64 | custom fusion | bytes 1376768 | tf_op jit(solution)/shard_map/scatter | solution.py:133
  994.7 7.3 all-to-all-start.1
  1002.1 23.9 %all-to-all-done.1 = bf16[32,112,192]{1,2,0:T(8,128)(2,1)} async-done(((bf16[32,112,192]{1,2,0:T(8,128)(2,1)}), bf16[32,112,192]{1,2,0:T(8,128)(2,1)}, u32[]{:S(2)}, u32[]{:S(2)}) %all-to-all-start.1) | async-done | bytes 1376288 | tf_op jit(solution)/shard_map/all_to_all | solution.py:137
  (393 shorter events, 404.3 us)
Async XLA Ops:
  7.2 647.4 %copy-start = (bf16[512,3200]{1,0:T(8,128)(2,1)S(1)}, bf16[512,3200]{1,0:T(8,128)(2,1)}, u32[]{:S(2)}) copy-start(bf16[512,3200]{1,0:T(8,128)(2,1)} %param.23) | copy-start | bytes 9830404
  7.2 201.5 %all-gather.3.cloned.1.call-start = ((), (), s32[]{:S(2)}) async-start(), calls=%async_computation.2 | async-start | bytes 12976128 | tf_op jit(solution)/shard_map/all_gather | solution.py:90
  7.2 2.6 copy-start.2
  9.8 4.3 copy-start.12
  24.3 184.4 %all-to-all-start = ((bf16[32,384,512]{2,1,0:T(8,128)(2,1)}), bf16[32,384,512]{2,1,0:T(8,128)(2,1)}, u32[]{:S(2)}, u32[]{:S(2)}) async-start(bf16[32,384,512]{2,1,0:T(8,128)(2,1)} %tile.2), calls=%async_computation | async-start | bytes 25165824 | tf_op jit(solution)/shard_map/all_to_all | solution.py:93
  31.8 691.8 %all-reduce.3.cloned.1.call-start = ((), (), s32[]{:S(2)}) async-start(), calls=%async_computation.3 | async-start | bytes 4915200 | tf_op jit(solution)/shard_map/psum | solution.py:113
  31.9 5.2 copy-start.13
  654.6 69.0 %copy-start.5 = (f32[3200]{0:T(1024)S(1)}, f32[3200]{0:T(1024)}, u32[]{:S(2)}) copy-start(f32[3200]{0:T(1024)} %param.24) | copy-start | bytes 38404
  657.6 66.0 %copy-start.3 = (bf16[384,3200]{1,0:T(8,128)(2,1)S(1)}, bf16[384,3200]{1,0:T(8,128)(2,1)}, u32[]{:S(2)}) copy-start(bf16[384,3200]{1,0:T(8,128)(2,1)} %param.18) | copy-start | bytes 7372804
  657.6 247.8 %all-gather.5.cloned.1.call-start = ((), (), s32[]{:S(2)}) async-start(), calls=%async_computation.4 | async-start | bytes 20275200 | tf_op jit(solution)/shard_map/all_gather | solution.py:123
  823.2 2.1 copy-start.6
  823.2 2.1 copy-start.7
  826.4 93.4 %copy-start.4 = (bf16[512,192]{0,1:T(8,128)(2,1)S(1)}, bf16[512,192]{0,1:T(8,128)(2,1)}, u32[]{:S(2)}) copy-start(bf16[512,192]{0,1:T(8,128)(2,1)} %param.29) | copy-start | bytes 589828
  826.4 93.6 %copy-start.10 = (s32[512]{0:T(512)S(1)}, s32[512]{0:T(512)}, u32[]{:S(2)}) copy-start(s32[512]{0:T(512)} %param.33) | copy-start | bytes 6148
  826.4 93.6 %copy-start.8 = (s32[3072]{0:T(1024)S(1)}, s32[3072]{0:T(1024)}, u32[]{:S(2)}) copy-start(s32[3072]{0:T(1024)} %param.32) | copy-start | bytes 36868
  826.5 139.8 %copy-start.11 = (f32[192]{0:T(256)S(1)}, f32[192]{0:T(256)}, u32[]{:S(2)}) copy-start(f32[192]{0:T(256)} %param.28) | copy-start | bytes 2308
  826.5 139.8 %all-reduce.5.cloned.1.call-start = ((), (), s32[]{:S(2)}) async-start(), calls=%async_computation.5 | async-start | bytes 2359296 | tf_op jit(solution)/shard_map/psum | solution.py:128
  994.7 33.5 %copy-start.9 = (f32[1536]{0:T(1024)S(1)}, f32[1536]{0:T(1024)}, u32[]{:S(2)}) copy-start(f32[1536]{0:T(1024)} %param.30) | copy-start | bytes 18436
  994.7 31.3 %all-to-all-start.1 = ((bf16[32,112,192]{1,2,0:T(8,128)(2,1)}), bf16[32,112,192]{1,2,0:T(8,128)(2,1)}, u32[]{:S(2)}, u32[]{:S(2)}) async-start(bf16[32,112,192]{1,2,0:T(8,128)(2,1)} %copy.89), calls=%async_computation.1 | async-start | bytes 3145728 | tf_op jit(solution)/shard_map/all_to_all | solution.py:137
  1002.0 32.0 %copy-start.1 = (bf16[512,3200]{1,0:T(8,128)(2,1)S(1)}, bf16[512,3200]{1,0:T(8,128)(2,1)}, u32[]{:S(2)}) copy-start(bf16[512,3200]{1,0:T(8,128)(2,1)} %param.23) | copy-start | bytes 9830404
Sparse Core Ops, SparseCore 0:
  14.2 190.0 all-gather.2
  657.7 65.8 all-reduce.2
  826.5 78.7 all-gather.4
  920.0 46.2 all-reduce.4
